TPU v7x, 256 devices: a whole 4x4x8 slice. The times are simulated.
256 devices in a mesh: chan: 32 (over x, z), tile: 8 (over y, core).
Axes of the slice: x: 4, y: 4, z: 8, core: 2. Of those that a mesh axis runs over, the one named last changes fastest.
Arguments:
- voltage: float32 [2, 64, 512, 1024], P(None, 'tile', 'chan'), may hold values from -6 to 6
- fir_taps: float32 [4, 1024], replicated, may hold values from -3 to 3
- tile_slot: int32 [10], replicated, may hold values from 0 to 15, as said below
- tile_blocks: int32 [10, 2], replicated, may hold values from 0 to 3, as said below
Outputs:
- visibility: float32 [16, 1024, 2, 128, 128], P('tile', 'chan')
Inputs may be any that keep to these rules, and one draw needn't show every extreme that they name: `tile_slot`: the values are distinct; slot g belongs to device g // 2 of the tile axis. Every device of the tile axis holds at least one tile and at most 2, some exactly 2, and a device's tiles fill its lowest slots. `tile_blocks`: the unordered pairs of the rows are the 10 pairs of blocks p <= q, each once; a row may name its pair in either order.
All inputs are finite; a program needn't handle non-finite values.
Results may differ from a plain program's by a relative error of at most 0.0001.
Values sent between devices are 32-bit elements; how exact they have to be, the bound alone decides.
A program may use at most 64 MiB of HBM per device.

v0:
```python
import functools
import math

import jax
import jax.numpy as jnp
import ml_dtypes
import numpy as np
from jax import lax
from jax.experimental import pallas as pl
from jax.experimental.pallas import tpu as pltpu
from jax.sharding import PartitionSpec as P

MESH = pl.DeviceIdType.MESH
BLOCK = 128
RADIX = 4
HALVES = 2


def dft_tables(channels, scale):
    inner = channels // RADIX
    k2 = np.arange(inner)
    f2 = np.arange(inner)
    tables = []
    for f1 in range(RADIX):
        phase = (k2[None, :] * (RADIX * f2[:, None] + f1)) % channels * (2.0 * math.pi / channels)
        both = np.concatenate([np.cos(phase), np.sin(phase)], axis=1) * scale
        head = both.astype(ml_dtypes.bfloat16)
        tail = (both - head.astype(np.float64)).astype(ml_dtypes.bfloat16)
        tables.append(np.stack([head, tail]))
    return np.stack(tables)


def head_tail(value):
    head = value.astype(jnp.bfloat16)
    return head, (value - head.astype(jnp.float32)).astype(jnp.bfloat16)


def turn_lanes(value):
    row = lax.broadcasted_iota(jnp.int32, value.shape, 0)
    lane = lax.broadcasted_iota(jnp.int32, value.shape, 1) // 16
    for bit in range(3):
        step = 1 << bit
        row_bit = (row // step) % 2
        lane_bit = (lane // step) % 2
        up = pltpu.roll(pltpu.roll(value, 16 * step, 1), 8 - step, 0)
        if bit == 2:
            down = up
        else:
            down = pltpu.roll(pltpu.roll(value, 128 - 16 * step, 1), step, 0)
        value = jnp.where(row_bit == lane_bit, value, jnp.where(row_bit == 0, up, down))
    return value


def turn_kernel(
    chans, tiles, v_hbm, taps_ref, tab_hbm, out_hbm,
    v, tab, u_head, u_tail, sbuf, rbuf, gbuf,
    load_sem, hist_sem, turn_send, turn_recv, y_send, y_recv, out_sem,
):
    c = lax.axis_index("chan")
    t = lax.axis_index("tile")
    chunks = sbuf.shape[0]

    barrier = pltpu.get_barrier_semaphore()

    @pl.loop(1, chans)
    def _(i):
        pl.semaphore_signal(barrier, inc=1, device_id=(lax.rem(c + i, chans), t), device_id_type=MESH)

    for step in (1, 2, tiles - 1, tiles - 2):
        pl.semaphore_signal(barrier, inc=1, device_id=(c, lax.rem(t + step, tiles)), device_id_type=MESH)

    up = lax.rem(t + 2, tiles)
    down = lax.rem(t + tiles - 2, tiles)
    far = lax.rem(t + 4, tiles)
    partner = t + 1 - 2 * lax.rem(t, 2)
    previous = lax.rem(t + tiles - 1, tiles)

    load_v = pltpu.make_async_copy(v_hbm, v.at[:, pl.ds(0, 8)], load_sem.at[0])
    load_tab = pltpu.make_async_copy(tab_hbm, tab, load_sem.at[1])
    load_v.start()
    load_tab.start()

    def filter_half(half):
        @pl.loop(0, 4)
        def _(s):
            for kb in range(2):
                part = []
                for k1 in range(RADIX):
                    lanes = pl.ds(k1 * 256 + kb * 128, 128)
                    for ri in range(2):
                        total = jnp.zeros((16, 128), jnp.float32)
                        for tap in range(4):
                            total = total + taps_ref[pl.ds(tap, 1), lanes] * v[ri, half * 4 + s + tap, :, lanes]
                        part.append(total)
                r = part[0::2]
                m = part[1::2]
                sum_r, sum_m = r[0] + r[2], m[0] + m[2]
                dif_r, dif_m = r[0] - r[2], m[0] - m[2]
                odd_r, odd_m = r[1] + r[3], m[1] + m[3]
                odf_r, odf_m = r[1] - r[3], m[1] - m[3]
                turned = (
                    (sum_r + odd_r, sum_m + odd_m),
                    (dif_r + odf_m, dif_m - odf_r),
                    (sum_r - odd_r, sum_m - odd_m),
                    (dif_r - odf_m, dif_m + odf_r),
                )
                row = pl.multiple_of(s * 16, 16)
                for f1 in range(RADIX):
                    re, im = turned[f1]
                    re_h, re_t = head_tail(re)
                    im_h, im_t = head_tail(im)
                    first = pl.ds(kb * 128, 128)
                    second = pl.ds(256 + kb * 128, 128)
                    u_head[f1, pl.ds(row, 16), first] = re_h
                    u_tail[f1, pl.ds(row, 16), first] = re_t
                    u_head[f1, pl.ds(row, 16), second] = im_h
                    u_tail[f1, pl.ds(row, 16), second] = im_t
                    u_head[f1, pl.ds(64 + row, 16), first] = im_h
                    u_tail[f1, pl.ds(64 + row, 16), first] = im_t
                    u_head[f1, pl.ds(64 + row, 16), second] = -re_h
                    u_tail[f1, pl.ds(64 + row, 16), second] = -re_t

    def transform(n):
        f1 = n % RADIX
        dims = (((1,), (1,)), ((), ()))
        dot = functools.partial(lax.dot_general, dimension_numbers=dims, preferred_element_type=jnp.float32)
        head, tail = u_head[f1], u_tail[f1]
        sbuf[n] = dot(tab[f1, 0], tail) + dot(tab[f1, 1], head) + dot(tab[f1, 0], head)

    def turn_copy(n, to):
        return pltpu.make_async_remote_copy(
            src_ref=sbuf.at[n, pl.ds(pl.multiple_of(to * 8, 8), 8)],
            dst_ref=rbuf.at[n, pl.ds(pl.multiple_of(c * 8, 8), 8)],
            send_sem=turn_send.at[n],
            recv_sem=turn_recv.at[n],
            device_id=(to, t),
            device_id_type=MESH,
        )

    def turn_start(n):
        @pl.loop(1, chans)
        def _(i):
            turn_copy(n, lax.rem(c + i, chans)).start()

    def turn_wait(n, sem):
        rows = pl.ds(0, (chans - 1) * 8)
        pltpu.make_async_copy(sbuf.at[n, rows], rbuf.at[n, rows], sem.at[n]).wait()

    def relay(n):
        turn_wait(n, turn_recv)
        mine = pl.ds(pl.multiple_of(c * 8, 8), 8)
        rbuf[n, mine] = sbuf[n, mine]

        @pl.loop(0, 8)
        def _(j):
            for a in range(4):
                gbuf[n, t, j, :, pl.ds(a * 128, 128)] = turn_lanes(rbuf[n, pl.ds(64 * a + j, 8, stride=8), :])

    def y_copy(n, block, to, send, recv):
        return pltpu.make_async_remote_copy(
            src_ref=gbuf.at[n, block],
            dst_ref=gbuf.at[n, block],
            send_sem=y_send.at[n, send],
            recv_sem=y_recv.at[n, recv],
            device_id=(c, to),
            device_id_type=MESH,
        )

    def own_copies(n):
        return [y_copy(n, t, up, 0, 0), y_copy(n, t, down, 1, 1), y_copy(n, t, partner, 2, 3)]

    def near_copies(n):
        across = y_copy(n, down, up, 3, 2) if n % 2 == 0 else y_copy(n, up, down, 3, 2)
        return [across, y_copy(n, down, partner, 4, 4), y_copy(n, up, partner, 5, 5)]

    def far_copies(n):
        return [y_copy(n, far, partner, 6, 6)]

    def start_own(n):
        for copy in own_copies(n):
            copy.start()

    def start_near(n):
        own = own_copies(n)
        own[0].wait_recv()
        own[1].wait_recv()
        for copy in near_copies(n):
            copy.start()

    def start_far(n):
        near_copies(n)[0].wait_recv()
        far_copies(n)[0].start()

    def finish(n):
        own_copies(n)[2].wait_recv()
        near = near_copies(n)
        near[1].wait_recv()
        near[2].wait_recv()
        far_copies(n)[0].wait_recv()
        pltpu.make_async_copy(gbuf.at[n], out_hbm.at[n], out_sem.at[n]).start()

    history = pltpu.make_async_remote_copy(
        src_ref=v_hbm.at[:, pl.ds(0, 3)],
        dst_ref=v.at[:, pl.ds(8, 3)],
        send_sem=hist_sem.at[0],
        recv_sem=hist_sem.at[1],
        device_id=(c, previous),
        device_id_type=MESH,
    )

    load_v.wait()
    filter_half(0)
    load_tab.wait()
    transform(0)
    pl.semaphore_wait(barrier, chans - 1 + 4)
    history.start()
    half_chunks = chunks // HALVES
    turn_start(0)
    for n in range(1, half_chunks):
        transform(n)
        turn_start(n)
    history.wait_recv()

    @pl.when(t == tiles - 1)
    def _():
        for ri in range(2):
            for frame in range(8, 11):
                v[ri, frame] = jnp.zeros(v.shape[2:], jnp.float32)

    filter_half(1)
    for n in range(half_chunks, chunks):
        transform(n)
        turn_start(n)
    for n in range(chunks + 3):
        if n < chunks:
            relay(n)
            start_own(n)
        if 0 <= n - 1 < chunks:
            start_near(n - 1)
        if 0 <= n - 2 < chunks:
            start_far(n - 2)
        if 0 <= n - 3 < chunks:
            finish(n - 3)
    history.wait_send()
    for n in range(chunks):
        turn_wait(n, turn_send)
        for copy in own_copies(n) + near_copies(n) + far_copies(n):
            copy.wait_send()
        pltpu.make_async_copy(gbuf.at[n], out_hbm.at[n], out_sem.at[n]).wait()


def gather_spectra(voltage, fir_taps, tables, chans, tiles):
    frames, inputs, samples = voltage.shape[1:]
    chunks = HALVES * RADIX
    f32 = jnp.float32
    return pl.pallas_call(
        functools.partial(turn_kernel, chans, tiles),
        out_shape=jax.ShapeDtypeStruct((chunks, tiles, 8, 8, 512), f32),
        in_specs=[
            pl.BlockSpec(memory_space=pl.ANY),
            pl.BlockSpec(memory_space=pltpu.VMEM),
            pl.BlockSpec(memory_space=pl.ANY),
        ],
        out_specs=pl.BlockSpec(memory_space=pl.ANY),
        scratch_shapes=[
            pltpu.VMEM((2, frames + 3, inputs, samples), f32),
            pltpu.VMEM(tables.shape, jnp.bfloat16),
            pltpu.VMEM((RADIX, 128, 512), jnp.bfloat16),
            pltpu.VMEM((RADIX, 128, 512), jnp.bfloat16),
            pltpu.VMEM((chunks, 256, 128), f32),
            pltpu.VMEM((chunks, 256, 128), f32),
            pltpu.VMEM((chunks, tiles, 8, 8, 512), f32),
            pltpu.SemaphoreType.DMA((2,)),
            pltpu.SemaphoreType.DMA((2,)),
            pltpu.SemaphoreType.DMA((chunks,)),
            pltpu.SemaphoreType.DMA((chunks,)),
            pltpu.SemaphoreType.DMA((chunks, 7)),
            pltpu.SemaphoreType.DMA((chunks, 7)),
            pltpu.SemaphoreType.DMA((chunks,)),
        ],
        compiler_params=pltpu.CompilerParams(collective_id=0, has_side_effects=True, vmem_limit_bytes=40 << 20),
        name="turn",
    )(voltage, fir_taps, tables)


def tile_kernel(slot_ref, blocks_ref, x_ref, o_ref):
    t = lax.axis_index("tile")
    tile_count = slot_ref.shape[0]
    step = x_ref.shape[3]
    sign = jnp.where(lax.broadcasted_iota(jnp.int32, (16, 8, BLOCK), 1) < 4, -1.0, 1.0)
    for slot in range(o_ref.shape[0]):
        found = jnp.int32(0)
        row_block = jnp.int32(0)
        col_block = jnp.int32(0)
        for r in range(tile_count):
            hit = (slot_ref[r] == t * o_ref.shape[0] + slot).astype(jnp.int32)
            found += hit
            row_block += hit * blocks_ref[r, 0]
            col_block += hit * blocks_ref[r, 1]
        rows = pl.ds(pl.multiple_of(row_block * BLOCK, BLOCK), BLOCK)
        cols = pl.ds(pl.multiple_of(col_block * BLOCK, BLOCK), BLOCK)

        @pl.when(found > 0)
        def _():
            @pl.loop(0, step)
            def _(j):
                left = x_ref[:, 0, :, j, :, rows].reshape(BLOCK, BLOCK)
                right = x_ref[:, 0, :, j, :, cols].reshape(16, 8, BLOCK)
                other = (pltpu.roll(right, 4, 1) * sign).reshape(BLOCK, BLOCK)
                right = right.reshape(BLOCK, BLOCK)
                both = jnp.concatenate([right, other], axis=1)
                left_head, left_tail = head_tail(left.T)
                both_head, both_tail = head_tail(both)
                dot = functools.partial(jnp.dot, preferred_element_type=jnp.float32)
                total = dot(left_tail, both_head) + dot(left_head, both_tail) + dot(left_head, both_head)
                o_ref[slot, j, 0, 0] = total[:, :BLOCK]
                o_ref[slot, j, 0, 1] = total[:, BLOCK:]

        @pl.when(found == 0)
        def _():
            o_ref[slot] = jnp.zeros(o_ref.shape[1:], jnp.float32)


def make_tiles(spectra, tile_slot, tile_blocks, slots, step=4):
    tiles = spectra.shape[1]
    spectra = spectra.reshape(HALVES, RADIX, tiles, 8, 8, 512)
    out = pl.pallas_call(
        tile_kernel,
        grid=(RADIX, 8 // step),
        out_shape=jax.ShapeDtypeStruct((slots, 8, RADIX, 2, BLOCK, BLOCK), jnp.float32),
        in_specs=[
            pl.BlockSpec(memory_space=pltpu.SMEM),
            pl.BlockSpec(memory_space=pltpu.SMEM),
            pl.BlockSpec((HALVES, 1, tiles, step, 8, 512), lambda f, j: (0, f, 0, j, 0, 0)),
        ],
        out_specs=pl.BlockSpec((slots, step, 1, 2, BLOCK, BLOCK), lambda f, j: (0, j, f, 0, 0, 0)),
        compiler_params=pltpu.CompilerParams(vmem_limit_bytes=32 << 20),
        name="tiles",
    )(tile_slot, tile_blocks, spectra)
    return out.reshape(slots, 8 * RADIX, 2, BLOCK, BLOCK)


def solution(mesh):
    chans, tiles = mesh.shape["chan"], mesh.shape["tile"]

    def body(voltage, fir_taps, tile_slot, tile_blocks):
        channels = voltage.shape[3]
        spectra_total = voltage.shape[1] * tiles
        slots = -(-tile_slot.shape[0] // tiles)
        tables = jnp.asarray(dft_tables(channels, 1.0 / math.sqrt(channels * spectra_total)))
        spectra = gather_spectra(voltage, fir_taps, tables, chans, tiles)
        return make_tiles(spectra, tile_slot, tile_blocks, slots)

    in_specs = (P(None, "tile", "chan", None), P(), P(), P())
    out_specs = P("tile", "chan", None, None, None)
    return jax.shard_map(body, mesh=mesh, in_specs=in_specs, out_specs=out_specs, check_vma=False)
```

profile of v0, /device:TPU:1, one launch (start us, length us, event | category | flops | bytes accessed | tf_op | source)
XLA Modules:
  0.0 85.6 jit_solution(7071410340983863756)
XLA Ops:
  0.0 0.0 copy-start.3
  0.0 0.8 copy.6.blocks_ref
  0.8 0.0 copy-start
  0.8 1.6 %copy-done = bf16[4,2,256,512]{3,2,1,0:T(8,128)(2,1)S(1)} copy-done((bf16[4,2,256,512]{3,2,1,0:T(8,128)(2,1)S(1)}, bf16[4,2,256,512]{3,2,1,0:T(8,128)(2,1)}, u32[]{:S(2)}) %copy-start) | copy-done | bytes 2097176
  2.4 0.0 copy-start.1
  2.4 1.2 %copy-done.1 = f32[2,8,16,1024]{3,2,1,0:T(8,128)S(1)} copy-done((f32[2,8,16,1024]{3,2,1,0:T(8,128)S(1)}, f32[2,8,16,1024]{3,2,1,0:T(8,128)}, u32[]{:S(2)}) %copy-start.1) | copy-done | bytes 1048600
  3.6 0.0 copy-start.2
  3.6 0.7 copy-done.2
  4.3 61.7 %turn.1 = f32[8,8,8,8,512]{4,3,2,1,0:T(8,128)S(1)} custom-call(f32[2,8,16,1024]{3,2,1,0:T(8,128)S(1)} %copy-done.1, f32[4,1024]{1,0:T(4,128)S(1)} %copy-done.2, bf16[4,2,256,512]{3,2,1,0:T(8,128)(2,1)S(1)} %copy-done), custom_call_target="tpu_custom_call" | custom-call | tf_op jit(solution)/shard_map/turn/pallas_call | solution.py:256
  66.0 0.0 copy-done.3
  66.0 19.6 %tiles.1 = f32[2,8,4,2,128,128]{5,4,3,2,1,0:T(8,128)} custom-call(s32[10]{0:T(128)S(1)} %copy-done.3, s32[10,2]{1,0:T(8,128)S(1)} %copy.6.blocks_ref, f32[2,4,8,8,8,512]{5,4,3,2,1,0:T(8,128)S(1)} %bitcast.2), custom_call_target="tpu_custom_call" | custom-call | tf_op jit(solution)/shard_map/tiles/pallas_call | solution.py:327
Async XLA Ops:
  0.0 66.0 %copy-start.3 = (s32[10]{0:T(128)S(1)}, s32[10]{0:T(128)}, u32[]{:S(2)}) copy-start(s32[10]{0:T(128)} %slot_ref.1) | copy-start | bytes 124
  0.8 1.6 %copy-start = (bf16[4,2,256,512]{3,2,1,0:T(8,128)(2,1)S(1)}, bf16[4,2,256,512]{3,2,1,0:T(8,128)(2,1)}, u32[]{:S(2)}) copy-start(bf16[4,2,256,512]{3,2,1,0:T(8,128)(2,1)} %constant.2.clone.tab_hbm) | copy-start | bytes 6291460
  2.4 1.2 %copy-start.1 = (f32[2,8,16,1024]{3,2,1,0:T(8,128)S(1)}, f32[2,8,16,1024]{3,2,1,0:T(8,128)}, u32[]{:S(2)}) copy-start(f32[2,8,16,1024]{3,2,1,0:T(8,128)} %v_hbm.1) | copy-start | bytes 3145732
  3.6 0.7 copy-start.2
where the time goes:
time: 87.2 us; the launch traced here: 85.6 us
  Pallas kernels  81.3 us (93%)
  local copies, waits for them, and re-layouts  4.32 us (5%)
    pallas_call x1, Pallas kernels, gather_spectra(): pl.pallas_call(functools.partial(turn_kernel, chans, tiles), out_shape=ja...  61.7 us
    pallas_call x1, Pallas kernels, make_tiles(): pl.pallas_call(tile_kernel, grid=(RADIX, 8 // step), out_shape=jax.ShapeD...  19.6 us
    unnamed x9, local copies, waits for them, and re-layouts  4.32 us

commit v1 on v0

--- a/solution.py
+++ b/solution.py
@@ -51,11 +51,46 @@
     return value
 
 
+def find_tile(slot_ref, blocks_ref, wanted):
+    found = jnp.int32(0)
+    row_block = jnp.int32(0)
+    col_block = jnp.int32(0)
+    for r in range(slot_ref.shape[0]):
+        hit = (slot_ref[r] == wanted).astype(jnp.int32)
+        found += hit
+        row_block += hit * blocks_ref[0, r]
+        col_block += hit * blocks_ref[1, r]
+    rows = pl.ds(pl.multiple_of(row_block * BLOCK, BLOCK), BLOCK)
+    cols = pl.ds(pl.multiple_of(col_block * BLOCK, BLOCK), BLOCK)
+    return found, rows, cols
+
+
+def pick_weights(slot_ref, blocks_ref, wanted, side, blocks):
+    weights = [jnp.float32(0)] * blocks
+    for r in range(slot_ref.shape[0]):
+        hit = slot_ref[r] == wanted
+        for block in range(blocks):
+            weights[block] += jnp.where(hit & (blocks_ref[side, r] == block), 1.0, 0.0)
+    return weights
+
+
+def correlate(left, right):
+    sign = jnp.where(lax.broadcasted_iota(jnp.int32, (16, 8, BLOCK), 1) < 4, -1.0, 1.0)
+    left = left.reshape(BLOCK, BLOCK)
+    other = (pltpu.roll(right, 4, 1) * sign).reshape(BLOCK, BLOCK)
+    both = jnp.concatenate([right.reshape(BLOCK, BLOCK), other], axis=1)
+    left_head, left_tail = head_tail(left.T)
+    both_head, both_tail = head_tail(both)
+    dot = functools.partial(jnp.dot, preferred_element_type=jnp.float32)
+    return dot(left_tail, both_head) + dot(left_head, both_tail) + dot(left_head, both_head)
+
+
 def turn_kernel(
-    chans, tiles, v_hbm, taps_ref, tab_hbm, out_hbm,
-    v, tab, u_head, u_tail, sbuf, rbuf, gbuf,
-    load_sem, hist_sem, turn_send, turn_recv, y_send, y_recv, out_sem,
+    chans, tiles, slots, v_hbm, taps_hbm, tab_hbm, slot_ref, blocks_ref, out_hbm, last_ref,
+    v, taps_ref, tab, u_head, u_tail, sbuf, rbuf, staged, *rest,
 ):
+    gbufs = rest[: HALVES * RADIX]
+    load_sem, hist_sem, turn_send, turn_recv, y_send, y_recv, out_sem = rest[HALVES * RADIX :]
     c = lax.axis_index("chan")
     t = lax.axis_index("tile")
     chunks = sbuf.shape[0]
@@ -77,8 +112,14 @@
 
     load_v = pltpu.make_async_copy(v_hbm, v.at[:, pl.ds(0, 8)], load_sem.at[0])
     load_tab = pltpu.make_async_copy(tab_hbm, tab, load_sem.at[1])
+    load_taps = pltpu.make_async_copy(taps_hbm, taps_ref, load_sem.at[2])
     load_v.start()
+    load_taps.start()
     load_tab.start()
+
+    weights = [
+        [pick_weights(slot_ref, blocks_ref, t * slots + slot, side, 4) for side in range(2)] for slot in range(slots)
+    ]
 
     def filter_half(half):
         @pl.loop(0, 4)
@@ -151,15 +192,14 @@
         mine = pl.ds(pl.multiple_of(c * 8, 8), 8)
         rbuf[n, mine] = sbuf[n, mine]
 
-        @pl.loop(0, 8)
-        def _(j):
+        for j in range(8):
             for a in range(4):
-                gbuf[n, t, j, :, pl.ds(a * 128, 128)] = turn_lanes(rbuf[n, pl.ds(64 * a + j, 8, stride=8), :])
+                gbufs[n][t, j, :, pl.ds(a * 128, 128)] = turn_lanes(rbuf[n, pl.ds(64 * a + j, 8, stride=8), :])
 
     def y_copy(n, block, to, send, recv):
         return pltpu.make_async_remote_copy(
-            src_ref=gbuf.at[n, block],
-            dst_ref=gbuf.at[n, block],
+            src_ref=gbufs[n].at[block],
+            dst_ref=gbufs[n].at[block],
             send_sem=y_send.at[n, send],
             recv_sem=y_recv.at[n, recv],
             device_id=(c, to),
@@ -197,7 +237,32 @@
         near[1].wait_recv()
         near[2].wait_recv()
         far_copies(n)[0].wait_recv()
-        pltpu.make_async_copy(gbuf.at[n], out_hbm.at[n], out_sem.at[n]).start()
+
+    def out_copy(f1):
+        return pltpu.make_async_copy(staged.at[f1], out_hbm.at[f1], out_sem.at[f1])
+
+    def last_copy(half):
+        n = half * RADIX + RADIX - 1
+        return pltpu.make_async_copy(gbufs[n], last_ref.at[half], out_sem.at[n])
+
+    def make_tiles(f1):
+        halves = [gbufs[half * RADIX + f1] for half in range(HALVES)]
+
+        @pl.loop(0, 8, step=2)
+        def _(first):
+            for more in range(2):
+                j = first + more
+                blocks = [
+                    jnp.concatenate([half[:, j, :, block * BLOCK : (block + 1) * BLOCK] for half in halves], axis=0)
+                    for block in range(4)
+                ]
+                for slot in range(slots):
+                    left, right = [sum(w * x for w, x in zip(side, blocks)) for side in weights[slot]]
+                    total = correlate(left, right)
+                    staged[f1, slot, j, 0] = total[:, :BLOCK]
+                    staged[f1, slot, j, 1] = total[:, BLOCK:]
+
+        out_copy(f1).start()
 
     history = pltpu.make_async_remote_copy(
         src_ref=v_hbm.at[:, pl.ds(0, 3)],
@@ -209,6 +274,7 @@
     )
 
     load_v.wait()
+    load_taps.wait()
     filter_half(0)
     load_tab.wait()
     transform(0)
@@ -219,6 +285,8 @@
     for n in range(1, half_chunks):
         transform(n)
         turn_start(n)
+    relay(0)
+    start_own(0)
     history.wait_recv()
 
     @pl.when(t == tiles - 1)
@@ -231,7 +299,7 @@
     for n in range(half_chunks, chunks):
         transform(n)
         turn_start(n)
-    for n in range(chunks + 3):
+    for n in range(1, chunks + 3):
         if n < chunks:
             relay(n)
             start_own(n)
@@ -239,38 +307,50 @@
             start_near(n - 1)
         if 0 <= n - 2 < chunks:
             start_far(n - 2)
-        if 0 <= n - 3 < chunks:
-            finish(n - 3)
+        done = n - 3
+        if 0 <= done < chunks:
+            finish(done)
+            half, f1 = done // RADIX, done % RADIX
+            if f1 == RADIX - 1:
+                last_copy(half).start()
+            elif half == HALVES - 1:
+                make_tiles(f1)
     history.wait_send()
     for n in range(chunks):
         turn_wait(n, turn_send)
         for copy in own_copies(n) + near_copies(n) + far_copies(n):
             copy.wait_send()
-        pltpu.make_async_copy(gbuf.at[n], out_hbm.at[n], out_sem.at[n]).wait()
-
-
-def gather_spectra(voltage, fir_taps, tables, chans, tiles):
+    for f1 in range(RADIX - 1):
+        out_copy(f1).wait()
+    for half in range(HALVES):
+        last_copy(half).wait()
+
+
+def early_tiles(voltage, fir_taps, tables, tile_slot, tile_blocks, chans, tiles, slots):
     frames, inputs, samples = voltage.shape[1:]
     chunks = HALVES * RADIX
     f32 = jnp.float32
+    any_space = pl.BlockSpec(memory_space=pl.ANY)
+    smem = pl.BlockSpec(memory_space=pltpu.SMEM)
     return pl.pallas_call(
-        functools.partial(turn_kernel, chans, tiles),
-        out_shape=jax.ShapeDtypeStruct((chunks, tiles, 8, 8, 512), f32),
-        in_specs=[
-            pl.BlockSpec(memory_space=pl.ANY),
-            pl.BlockSpec(memory_space=pltpu.VMEM),
-            pl.BlockSpec(memory_space=pl.ANY),
-        ],
-        out_specs=pl.BlockSpec(memory_space=pl.ANY),
+        functools.partial(turn_kernel, chans, tiles, slots),
+        out_shape=(
+            jax.ShapeDtypeStruct((RADIX - 1, slots, 8, 2, BLOCK, BLOCK), f32),
+            jax.ShapeDtypeStruct((HALVES, tiles, 8, 8, 512), f32),
+        ),
+        in_specs=[any_space, any_space, any_space, smem, smem],
+        out_specs=(any_space, any_space),
         scratch_shapes=[
             pltpu.VMEM((2, frames + 3, inputs, samples), f32),
+            pltpu.VMEM(fir_taps.shape, f32),
             pltpu.VMEM(tables.shape, jnp.bfloat16),
             pltpu.VMEM((RADIX, 128, 512), jnp.bfloat16),
             pltpu.VMEM((RADIX, 128, 512), jnp.bfloat16),
             pltpu.VMEM((chunks, 256, 128), f32),
             pltpu.VMEM((chunks, 256, 128), f32),
-            pltpu.VMEM((chunks, tiles, 8, 8, 512), f32),
-            pltpu.SemaphoreType.DMA((2,)),
+            pltpu.VMEM((RADIX - 1, slots, 8, 2, BLOCK, BLOCK), f32),
+            *[pltpu.VMEM((tiles, 8, 8, 512), f32) for _ in range(chunks)],
+            pltpu.SemaphoreType.DMA((3,)),
             pltpu.SemaphoreType.DMA((2,)),
             pltpu.SemaphoreType.DMA((chunks,)),
             pltpu.SemaphoreType.DMA((chunks,)),
@@ -278,66 +358,74 @@
             pltpu.SemaphoreType.DMA((chunks, 7)),
             pltpu.SemaphoreType.DMA((chunks,)),
         ],
-        compiler_params=pltpu.CompilerParams(collective_id=0, has_side_effects=True, vmem_limit_bytes=40 << 20),
+        compiler_params=pltpu.CompilerParams(collective_id=0, has_side_effects=True, vmem_limit_bytes=67_043_328),
         name="turn",
-    )(voltage, fir_taps, tables)
-
-
-def tile_kernel(slot_ref, blocks_ref, x_ref, o_ref):
+    )(voltage, fir_taps, tables, tile_slot, tile_blocks)
+
+
+def tile_kernel(slot_ref, blocks_ref, early_ref, spectra_ref, out_hbm, spectra, moved, staged, load_sem, move_sem, out_sem):
     t = lax.axis_index("tile")
-    tile_count = slot_ref.shape[0]
-    step = x_ref.shape[3]
-    sign = jnp.where(lax.broadcasted_iota(jnp.int32, (16, 8, BLOCK), 1) < 4, -1.0, 1.0)
-    for slot in range(o_ref.shape[0]):
-        found = jnp.int32(0)
-        row_block = jnp.int32(0)
-        col_block = jnp.int32(0)
-        for r in range(tile_count):
-            hit = (slot_ref[r] == t * o_ref.shape[0] + slot).astype(jnp.int32)
-            found += hit
-            row_block += hit * blocks_ref[r, 0]
-            col_block += hit * blocks_ref[r, 1]
-        rows = pl.ds(pl.multiple_of(row_block * BLOCK, BLOCK), BLOCK)
-        cols = pl.ds(pl.multiple_of(col_block * BLOCK, BLOCK), BLOCK)
+    slots, step = staged.shape[:2]
+    load = pltpu.make_async_copy(spectra_ref, spectra, load_sem)
+    load.start()
+    parts = [(f1, slot) for f1 in range(RADIX - 1) for slot in range(slots)]
+    moves = [pltpu.make_async_copy(early_ref.at[f1, slot], moved.at[f1, slot], move_sem.at[f1, slot]) for f1, slot in parts]
+    early = [pltpu.make_async_copy(moved.at[f1, slot], out_hbm.at[slot, :, f1], out_sem.at[f1, slot]) for f1, slot in parts]
+    for move in moves:
+        move.start()
+    load.wait()
+    halves = [spectra.at[half] for half in range(HALVES)]
+    late = []
+    ahead = len(parts) // slots
+    for slot in range(slots):
+        for move, copy in zip(moves[slot * ahead : (slot + 1) * ahead], early[slot * ahead : (slot + 1) * ahead]):
+            move.wait()
+            copy.start()
+        found, rows, cols = find_tile(slot_ref, blocks_ref, t * slots + slot)
 
         @pl.when(found > 0)
         def _():
-            @pl.loop(0, step)
-            def _(j):
-                left = x_ref[:, 0, :, j, :, rows].reshape(BLOCK, BLOCK)
-                right = x_ref[:, 0, :, j, :, cols].reshape(16, 8, BLOCK)
-                other = (pltpu.roll(right, 4, 1) * sign).reshape(BLOCK, BLOCK)
-                right = right.reshape(BLOCK, BLOCK)
-                both = jnp.concatenate([right, other], axis=1)
-                left_head, left_tail = head_tail(left.T)
-                both_head, both_tail = head_tail(both)
-                dot = functools.partial(jnp.dot, preferred_element_type=jnp.float32)
-                total = dot(left_tail, both_head) + dot(left_head, both_tail) + dot(left_head, both_head)
-                o_ref[slot, j, 0, 0] = total[:, :BLOCK]
-                o_ref[slot, j, 0, 1] = total[:, BLOCK:]
+            @pl.loop(0, step, step=4)
+            def _(first):
+                for more in range(4):
+                    j = first + more
+                    left, right = [
+                        jnp.concatenate([half[:, j, :, lanes] for half in halves], axis=0) for lanes in (rows, cols)
+                    ]
+                    total = correlate(left, right)
+                    staged[slot, j, 0] = total[:, :BLOCK]
+                    staged[slot, j, 1] = total[:, BLOCK:]
 
         @pl.when(found == 0)
         def _():
-            o_ref[slot] = jnp.zeros(o_ref.shape[1:], jnp.float32)
-
-
-def make_tiles(spectra, tile_slot, tile_blocks, slots, step=4):
-    tiles = spectra.shape[1]
-    spectra = spectra.reshape(HALVES, RADIX, tiles, 8, 8, 512)
-    out = pl.pallas_call(
+            staged[slot] = jnp.zeros(staged.shape[1:], jnp.float32)
+
+        late.append(pltpu.make_async_copy(staged.at[slot], out_hbm.at[slot, :, RADIX - 1], out_sem.at[RADIX - 1, slot]))
+        late[-1].start()
+    for copy in early + late:
+        copy.wait()
+
+
+def last_tiles(early, spectra, tile_slot, tile_blocks):
+    slots = early.shape[1]
+    smem = pl.BlockSpec(memory_space=pltpu.SMEM)
+    any_space = pl.BlockSpec(memory_space=pl.ANY)
+    return pl.pallas_call(
         tile_kernel,
-        grid=(RADIX, 8 // step),
         out_shape=jax.ShapeDtypeStruct((slots, 8, RADIX, 2, BLOCK, BLOCK), jnp.float32),
-        in_specs=[
-            pl.BlockSpec(memory_space=pltpu.SMEM),
-            pl.BlockSpec(memory_space=pltpu.SMEM),
-            pl.BlockSpec((HALVES, 1, tiles, step, 8, 512), lambda f, j: (0, f, 0, j, 0, 0)),
+        in_specs=[smem, smem, any_space, any_space],
+        out_specs=any_space,
+        scratch_shapes=[
+            pltpu.VMEM(spectra.shape, jnp.float32),
+            pltpu.VMEM(early.shape, jnp.float32),
+            pltpu.VMEM((slots, 8, 2, BLOCK, BLOCK), jnp.float32),
+            pltpu.SemaphoreType.DMA,
+            pltpu.SemaphoreType.DMA((RADIX - 1, slots)),
+            pltpu.SemaphoreType.DMA((RADIX, slots)),
         ],
-        out_specs=pl.BlockSpec((slots, step, 1, 2, BLOCK, BLOCK), lambda f, j: (0, j, f, 0, 0, 0)),
-        compiler_params=pltpu.CompilerParams(vmem_limit_bytes=32 << 20),
+        compiler_params=pltpu.CompilerParams(vmem_limit_bytes=67_043_328),
         name="tiles",
-    )(tile_slot, tile_blocks, spectra)
-    return out.reshape(slots, 8 * RADIX, 2, BLOCK, BLOCK)
+    )(tile_slot, tile_blocks, early, spectra)
 
 
 def solution(mesh):
@@ -347,9 +435,11 @@
         channels = voltage.shape[3]
         spectra_total = voltage.shape[1] * tiles
         slots = -(-tile_slot.shape[0] // tiles)
+        blocks = tile_blocks.T
         tables = jnp.asarray(dft_tables(channels, 1.0 / math.sqrt(channels * spectra_total)))
-        spectra = gather_spectra(voltage, fir_taps, tables, chans, tiles)
-        return make_tiles(spectra, tile_slot, tile_blocks, slots)
+        early, last = early_tiles(voltage, fir_taps, tables, tile_slot, blocks, chans, tiles, slots)
+        out = last_tiles(early, last, tile_slot, blocks)
+        return out.reshape(slots, 8 * RADIX, 2, BLOCK, BLOCK)
 
     in_specs = (P(None, "tile", "chan", None), P(), P(), P())
     out_specs = P("tile", "chan", None, None, None)

time: 87.2 us -> 72 us (0.83); the launches traced: 85.6 us -> 71.8 us
  Pallas kernels: 81.3 us -> 71.8 us
  local copies, waits for them, and re-layouts: 4.32 us -> 0 us
    pallas_call x2, Pallas kernels: 81.3 us -> 71.8 us  [the longest x1 64.5 us: early_tiles(): pl.pallas_call(functools.partial(turn_kernel, chans, tiles, slots), out_s...]
    unnamed x9 -> x0, local copies, waits for them, and re-layouts: 4.32 us -> none
where the time goes in v1:
time: 72 us; the launch traced here: 71.8 us
  Pallas kernels  71.8 us (100%)
    pallas_call x1, Pallas kernels, early_tiles(): pl.pallas_call(functools.partial(turn_kernel, chans, tiles, slots), out_s...  64.5 us
    pallas_call x1, Pallas kernels, last_tiles(): pl.pallas_call(tile_kernel, out_shape=jax.ShapeDtypeStruct((slots, 8, RAD...  7.31 us

profile of v1, /device:TPU:1, one launch (start us, length us, event | category | flops | bytes accessed | tf_op | source)
XLA Modules:
  0.0 71.8 jit_solution(2520701730164067969)
XLA Ops:
  0.0 64.5 %turn.1 = (f32[3,2,8,2,128,128]{5,4,3,2,1,0:T(8,128)}, f32[2,8,8,8,512]{4,3,2,1,0:T(8,128)}) custom-call(f32[2,8,16,1024]{3,2,1,0:T(8,128)} %v_hbm.1, f32[4,1024]{1,0:T(4,128)} %taps_hbm.1, bf16[4,2,256,512]{3,2,1,0:T(8,128)(2,1)} %constant.2.clone.tab_hbm, s32[10]{0:T(128)} %slot_ref.3, s32[2,10]{1,0:T(2,128)} %bitcast.2), custom_call_target="tpu_custom_call" | custom-call | tf_op jit(solution)/shard_map/turn/pallas_call | solution.py:335
  64.5 7.3 %tiles.1 = f32[2,8,4,2,128,128]{5,4,3,2,1,0:T(8,128)} custom-call(s32[10]{0:T(128)} %slot_ref.3, s32[2,10]{1,0:T(2,128)} %bitcast.3, f32[3,2,8,2,128,128]{5,4,3,2,1,0:T(8,128)} %get-tuple-element.7.early_ref, f32[2,8,8,8,512]{4,3,2,1,0:T(8,128)} %get-tuple-element.8.spectra_ref), custom_call_target="tpu_custom_call" | custom-call | tf_op jit(solution)/shard_map/tiles/pallas_call | solution.py:413

commit v2 on v1

--- a/solution.py
+++ b/solution.py
@@ -13,7 +13,10 @@
 MESH = pl.DeviceIdType.MESH
 BLOCK = 128
 RADIX = 4
+TURN_LIMIT = 40 << 20
+LAST_LIMIT = 40 << 20
 HALVES = 2
+AHEAD = 3
 
 
 def dft_tables(channels, scale):
@@ -179,9 +182,12 @@
         )
 
     def turn_start(n):
-        @pl.loop(1, chans)
+        turn_copy(n, lax.rem(c + chans // 2, chans)).start()
+
+        @pl.loop(1, chans // 2)
         def _(i):
             turn_copy(n, lax.rem(c + i, chans)).start()
+            turn_copy(n, lax.rem(c + chans - i, chans)).start()
 
     def turn_wait(n, sem):
         rows = pl.ds(0, (chans - 1) * 8)
@@ -196,47 +202,61 @@
             for a in range(4):
                 gbufs[n][t, j, :, pl.ds(a * 128, 128)] = turn_lanes(rbuf[n, pl.ds(64 * a + j, 8, stride=8), :])
 
-    def y_copy(n, block, to, send, recv):
+    def y_copy(n, block, to, slot, part=pl.ds(0, 8)):
         return pltpu.make_async_remote_copy(
-            src_ref=gbufs[n].at[block],
-            dst_ref=gbufs[n].at[block],
-            send_sem=y_send.at[n, send],
-            recv_sem=y_recv.at[n, recv],
+            src_ref=gbufs[n].at[block, part],
+            dst_ref=gbufs[n].at[block, part],
+            send_sem=y_send.at[n, slot],
+            recv_sem=y_recv.at[n, slot],
             device_id=(c, to),
             device_id_type=MESH,
         )
 
-    def own_copies(n):
-        return [y_copy(n, t, up, 0, 0), y_copy(n, t, down, 1, 1), y_copy(n, t, partner, 2, 3)]
-
-    def near_copies(n):
-        across = y_copy(n, down, up, 3, 2) if n % 2 == 0 else y_copy(n, up, down, 3, 2)
-        return [across, y_copy(n, down, partner, 4, 4), y_copy(n, up, partner, 5, 5)]
-
-    def far_copies(n):
-        return [y_copy(n, far, partner, 6, 6)]
+    low, high = pl.ds(0, 4), pl.ds(4, 4)
+
+    def y_copies(n):
+        return {
+            "up low": y_copy(n, t, up, 0, low),
+            "down high": y_copy(n, t, down, 1, high),
+            "up high": y_copy(n, t, up, 2, high),
+            "down low": y_copy(n, t, down, 3, low),
+            "own": y_copy(n, t, partner, 4),
+            "on low": y_copy(n, down, up, 5, low),
+            "on high": y_copy(n, up, down, 6, high),
+            "below": y_copy(n, down, partner, 7),
+            "above": y_copy(n, up, partner, 8),
+            "far": y_copy(n, far, partner, 9),
+        }
+
+    all_copies = [y_copies(n) for n in range(chunks)]
+
+    def y_start(n, *names):
+        for name in names:
+            all_copies[n][name].start()
+
+    def y_arrived(n, *names):
+        for name in names:
+            all_copies[n][name].wait_recv()
 
     def start_own(n):
-        for copy in own_copies(n):
-            copy.start()
+        y_start(n, "up low", "down high", "up high", "down low", "own")
 
     def start_near(n):
-        own = own_copies(n)
-        own[0].wait_recv()
-        own[1].wait_recv()
-        for copy in near_copies(n):
-            copy.start()
+        y_arrived(n, "up low")
+        y_start(n, "on low")
+        y_arrived(n, "down high")
+        y_start(n, "on high")
 
     def start_far(n):
-        near_copies(n)[0].wait_recv()
-        far_copies(n)[0].start()
+        y_arrived(n, "up high")
+        y_start(n, "below")
+        y_arrived(n, "down low")
+        y_start(n, "above")
+        y_arrived(n, "on low", "on high")
+        y_start(n, "far")
 
     def finish(n):
-        own_copies(n)[2].wait_recv()
-        near = near_copies(n)
-        near[1].wait_recv()
-        near[2].wait_recv()
-        far_copies(n)[0].wait_recv()
+        y_arrived(n, "own", "below", "above", "far")
 
     def out_copy(f1):
         return pltpu.make_async_copy(staged.at[f1], out_hbm.at[f1], out_sem.at[f1])
@@ -273,38 +293,38 @@
         device_id_type=MESH,
     )
 
+    def prepare(n):
+        if n == half_chunks:
+            history.wait_recv()
+
+            @pl.when(t == tiles - 1)
+            def _():
+                for ri in range(2):
+                    for frame in range(8, 11):
+                        v[ri, frame] = jnp.zeros(v.shape[2:], jnp.float32)
+
+            filter_half(1)
+        transform(n)
+        if n == 0:
+            pl.semaphore_wait(barrier, chans - 1 + 4)
+            history.start()
+        turn_start(n)
+
+    half_chunks = chunks // HALVES
     load_v.wait()
     load_taps.wait()
     filter_half(0)
     load_tab.wait()
-    transform(0)
-    pl.semaphore_wait(barrier, chans - 1 + 4)
-    history.start()
-    half_chunks = chunks // HALVES
-    turn_start(0)
-    for n in range(1, half_chunks):
-        transform(n)
-        turn_start(n)
-    relay(0)
-    start_own(0)
-    history.wait_recv()
-
-    @pl.when(t == tiles - 1)
-    def _():
-        for ri in range(2):
-            for frame in range(8, 11):
-                v[ri, frame] = jnp.zeros(v.shape[2:], jnp.float32)
-
-    filter_half(1)
-    for n in range(half_chunks, chunks):
-        transform(n)
-        turn_start(n)
-    for n in range(1, chunks + 3):
+    for n in range(AHEAD):
+        prepare(n)
+    for n in range(chunks + 3):
         if n < chunks:
             relay(n)
             start_own(n)
         if 0 <= n - 1 < chunks:
             start_near(n - 1)
+        if n + AHEAD < chunks:
+            prepare(n + AHEAD)
         if 0 <= n - 2 < chunks:
             start_far(n - 2)
         done = n - 3
@@ -318,12 +338,16 @@
     history.wait_send()
     for n in range(chunks):
         turn_wait(n, turn_send)
-        for copy in own_copies(n) + near_copies(n) + far_copies(n):
+        for copy in all_copies[n].values():
             copy.wait_send()
     for f1 in range(RADIX - 1):
         out_copy(f1).wait()
     for half in range(HALVES):
         last_copy(half).wait()
+
+
+def in_hbm(*arrays):
+    return [pltpu.with_memory_space_constraint(array, pltpu.HBM) for array in arrays]
 
 
 def early_tiles(voltage, fir_taps, tables, tile_slot, tile_blocks, chans, tiles, slots):
@@ -354,55 +378,46 @@
             pltpu.SemaphoreType.DMA((2,)),
             pltpu.SemaphoreType.DMA((chunks,)),
             pltpu.SemaphoreType.DMA((chunks,)),
-            pltpu.SemaphoreType.DMA((chunks, 7)),
-            pltpu.SemaphoreType.DMA((chunks, 7)),
+            pltpu.SemaphoreType.DMA((chunks, 10)),
+            pltpu.SemaphoreType.DMA((chunks, 10)),
             pltpu.SemaphoreType.DMA((chunks,)),
         ],
-        compiler_params=pltpu.CompilerParams(collective_id=0, has_side_effects=True, vmem_limit_bytes=67_043_328),
+        compiler_params=pltpu.CompilerParams(collective_id=0, has_side_effects=True, vmem_limit_bytes=TURN_LIMIT),
         name="turn",
-    )(voltage, fir_taps, tables, tile_slot, tile_blocks)
-
-
-def tile_kernel(slot_ref, blocks_ref, early_ref, spectra_ref, out_hbm, spectra, moved, staged, load_sem, move_sem, out_sem):
+    )(*in_hbm(voltage, fir_taps, tables, tile_slot, tile_blocks))
+
+
+def tile_kernel(slot_ref, blocks_ref, early_ref, spectra_ref, out_hbm, staged, out_sem):
     t = lax.axis_index("tile")
     slots, step = staged.shape[:2]
-    load = pltpu.make_async_copy(spectra_ref, spectra, load_sem)
-    load.start()
     parts = [(f1, slot) for f1 in range(RADIX - 1) for slot in range(slots)]
-    moves = [pltpu.make_async_copy(early_ref.at[f1, slot], moved.at[f1, slot], move_sem.at[f1, slot]) for f1, slot in parts]
-    early = [pltpu.make_async_copy(moved.at[f1, slot], out_hbm.at[slot, :, f1], out_sem.at[f1, slot]) for f1, slot in parts]
-    for move in moves:
-        move.start()
-    load.wait()
-    halves = [spectra.at[half] for half in range(HALVES)]
-    late = []
-    ahead = len(parts) // slots
+    copies = []
+    for i, (f1, slot) in enumerate(parts):
+        copies.append(pltpu.make_async_copy(early_ref.at[f1, slot], out_hbm.at[slot, :, f1], out_sem.at[i]))
+        copies[-1].start()
+    halves = [spectra_ref.at[half] for half in range(HALVES)]
     for slot in range(slots):
-        for move, copy in zip(moves[slot * ahead : (slot + 1) * ahead], early[slot * ahead : (slot + 1) * ahead]):
-            move.wait()
-            copy.start()
         found, rows, cols = find_tile(slot_ref, blocks_ref, t * slots + slot)
 
         @pl.when(found > 0)
         def _():
-            @pl.loop(0, step, step=4)
-            def _(first):
-                for more in range(4):
-                    j = first + more
-                    left, right = [
-                        jnp.concatenate([half[:, j, :, lanes] for half in halves], axis=0) for lanes in (rows, cols)
-                    ]
-                    total = correlate(left, right)
-                    staged[slot, j, 0] = total[:, :BLOCK]
-                    staged[slot, j, 1] = total[:, BLOCK:]
+            for j in range(step):
+                left, right = [
+                    jnp.concatenate([half[:, j, :, lanes] for half in halves], axis=0) for lanes in (rows, cols)
+                ]
+                total = correlate(left, right)
+                staged[slot, j, 0] = total[:, :BLOCK]
+                staged[slot, j, 1] = total[:, BLOCK:]
 
         @pl.when(found == 0)
         def _():
             staged[slot] = jnp.zeros(staged.shape[1:], jnp.float32)
 
-        late.append(pltpu.make_async_copy(staged.at[slot], out_hbm.at[slot, :, RADIX - 1], out_sem.at[RADIX - 1, slot]))
-        late[-1].start()
-    for copy in early + late:
+        copies.append(
+            pltpu.make_async_copy(staged.at[slot], out_hbm.at[slot, :, RADIX - 1], out_sem.at[len(parts) + slot])
+        )
+        copies[-1].start()
+    for copy in copies:
         copy.wait()
 
 
@@ -413,19 +428,15 @@
     return pl.pallas_call(
         tile_kernel,
         out_shape=jax.ShapeDtypeStruct((slots, 8, RADIX, 2, BLOCK, BLOCK), jnp.float32),
-        in_specs=[smem, smem, any_space, any_space],
+        in_specs=[smem, smem, any_space, pl.BlockSpec(memory_space=pltpu.VMEM)],
         out_specs=any_space,
         scratch_shapes=[
-            pltpu.VMEM(spectra.shape, jnp.float32),
-            pltpu.VMEM(early.shape, jnp.float32),
             pltpu.VMEM((slots, 8, 2, BLOCK, BLOCK), jnp.float32),
-            pltpu.SemaphoreType.DMA,
-            pltpu.SemaphoreType.DMA((RADIX - 1, slots)),
-            pltpu.SemaphoreType.DMA((RADIX, slots)),
+            pltpu.SemaphoreType.DMA((RADIX * slots,)),
         ],
-        compiler_params=pltpu.CompilerParams(vmem_limit_bytes=67_043_328),
+        compiler_params=pltpu.CompilerParams(vmem_limit_bytes=LAST_LIMIT),
         name="tiles",
-    )(tile_slot, tile_blocks, early, spectra)
+    )(*in_hbm(tile_slot, tile_blocks), early, spectra)
 
 
 def solution(mesh):

time: 72 us -> 63.7 us (0.88)
  Pallas kernels: 71.8 us -> 63.6 us
    pallas_call x1, Pallas kernels: 64.5 us -> 59.5 us  [early_tiles(): pl.pallas_call(functools.partial(turn_kernel, chans, tiles, slots), out_s...]
    pallas_call x1, Pallas kernels: 7.31 us -> 4.07 us  [last_tiles(): pl.pallas_call(tile_kernel, out_shape=jax.ShapeDtypeStruct((slots, 8, RAD...]
where the time goes in v2:
time: 63.7 us; the launch traced here: 63.6 us
  Pallas kernels  63.6 us (100%)
    pallas_call x1, Pallas kernels, early_tiles(): pl.pallas_call(functools.partial(turn_kernel, chans, tiles, slots), out_s...  59.5 us
    pallas_call x1, Pallas kernels, last_tiles(): pl.pallas_call(tile_kernel, out_shape=jax.ShapeDtypeStruct((slots, 8, RAD...  4.07 us

profile of v2, /device:TPU:1, one launch (start us, length us, event | category | flops | bytes accessed | tf_op | source)
XLA Modules:
  0.0 63.6 jit_solution(18254070695408143756)
XLA Ops:
  0.0 59.5 %turn.1 = (f32[3,2,8,2,128,128]{5,4,3,2,1,0:T(8,128)S(1)}, f32[2,8,8,8,512]{4,3,2,1,0:T(8,128)S(1)}) custom-call(f32[2,8,16,1024]{3,2,1,0:T(8,128)} %v_hbm.1, f32[4,1024]{1,0:T(4,128)} %taps_hbm.1, bf16[4,2,256,512]{3,2,1,0:T(8,128)(2,1)} %constant.2.clone.tab_hbm, s32[10]{0:T(128)} %slot_ref.3, s32[2,10]{1,0:T(2,128)} %bitcast.2), custom_call_target="tpu_custom_call" | custom-call | tf_op jit(solution)/shard_map/turn/pallas_call | solution.py:359
  59.5 4.1 %tiles.1 = f32[2,8,4,2,128,128]{5,4,3,2,1,0:T(8,128)} custom-call(s32[10]{0:T(128)} %slot_ref.3, s32[2,10]{1,0:T(2,128)} %bitcast.3, f32[3,2,8,2,128,128]{5,4,3,2,1,0:T(8,128)S(1)} %get-tuple-element.7.early_ref, f32[2,8,8,8,512]{4,3,2,1,0:T(8,128)S(1)} %get-tuple-element.8.spectra_ref), custom_call_target="tpu_custom_call" | custom-call | tf_op jit(solution)/shard_map/tiles/pallas_call | solution.py:428

commit v3 on v2

--- a/solution.py
+++ b/solution.py
@@ -16,6 +16,7 @@
 TURN_LIMIT = 40 << 20
 LAST_LIMIT = 40 << 20
 HALVES = 2
+SPREAD = 3
 AHEAD = 3
 
 
@@ -90,7 +91,7 @@
 
 def turn_kernel(
     chans, tiles, slots, v_hbm, taps_hbm, tab_hbm, slot_ref, blocks_ref, out_hbm, last_ref,
-    v, taps_ref, tab, u_head, u_tail, sbuf, rbuf, staged, *rest,
+    v, taps_ref, tab, u_head, u_tail, sbuf, rbuf, bsend, brecv, staged, *rest,
 ):
     gbufs = rest[: HALVES * RADIX]
     load_sem, hist_sem, turn_send, turn_recv, y_send, y_recv, out_sem = rest[HALVES * RADIX :]
@@ -119,10 +120,6 @@
     load_v.start()
     load_taps.start()
     load_tab.start()
-
-    weights = [
-        [pick_weights(slot_ref, blocks_ref, t * slots + slot, side, 4) for side in range(2)] for slot in range(slots)
-    ]
 
     def filter_half(half):
         @pl.loop(0, 4)
@@ -169,43 +166,47 @@
         dims = (((1,), (1,)), ((), ()))
         dot = functools.partial(lax.dot_general, dimension_numbers=dims, preferred_element_type=jnp.float32)
         head, tail = u_head[f1], u_tail[f1]
-        sbuf[n] = dot(tab[f1, 0], tail) + dot(tab[f1, 1], head) + dot(tab[f1, 0], head)
-
-    def turn_copy(n, to):
+        spectra = dot(tab[f1, 0], tail) + dot(tab[f1, 1], head) + dot(tab[f1, 0], head)
+        if n == SPREAD:
+            bsend[lax.div(t, 2)] = spectra
+        else:
+            sbuf[n] = spectra
+
+    def turn_copy(source, target, sem, to):
         return pltpu.make_async_remote_copy(
-            src_ref=sbuf.at[n, pl.ds(pl.multiple_of(to * 8, 8), 8)],
-            dst_ref=rbuf.at[n, pl.ds(pl.multiple_of(c * 8, 8), 8)],
-            send_sem=turn_send.at[n],
-            recv_sem=turn_recv.at[n],
+            src_ref=source.at[pl.ds(pl.multiple_of(to * 8, 8), 8)],
+            dst_ref=target.at[pl.ds(pl.multiple_of(c * 8, 8), 8)],
+            send_sem=turn_send.at[sem],
+            recv_sem=turn_recv.at[sem],
             device_id=(to, t),
             device_id_type=MESH,
         )
 
-    def turn_start(n):
-        turn_copy(n, lax.rem(c + chans // 2, chans)).start()
+    def turn_start(source, target, sem):
+        turn_copy(source, target, sem, lax.rem(c + chans // 2, chans)).start()
 
         @pl.loop(1, chans // 2)
         def _(i):
-            turn_copy(n, lax.rem(c + i, chans)).start()
-            turn_copy(n, lax.rem(c + chans - i, chans)).start()
-
-    def turn_wait(n, sem):
+            turn_copy(source, target, sem, lax.rem(c + i, chans)).start()
+            turn_copy(source, target, sem, lax.rem(c + chans - i, chans)).start()
+
+    def turn_wait(source, target, sems, sem):
         rows = pl.ds(0, (chans - 1) * 8)
-        pltpu.make_async_copy(sbuf.at[n, rows], rbuf.at[n, rows], sem.at[n]).wait()
-
-    def relay(n):
-        turn_wait(n, turn_recv)
+        pltpu.make_async_copy(source.at[rows], target.at[rows], sems.at[sem]).wait()
+
+    def relay(source, target, sem, n, block):
+        turn_wait(source, target, turn_recv, sem)
         mine = pl.ds(pl.multiple_of(c * 8, 8), 8)
-        rbuf[n, mine] = sbuf[n, mine]
-
+        target[mine] = source[mine]
         for j in range(8):
             for a in range(4):
-                gbufs[n][t, j, :, pl.ds(a * 128, 128)] = turn_lanes(rbuf[n, pl.ds(64 * a + j, 8, stride=8), :])
+                gbufs[n][block, j, :, pl.ds(a * 128, 128)] = turn_lanes(target[pl.ds(64 * a + j, 8, stride=8), :])
 
     def y_copy(n, block, to, slot, part=pl.ds(0, 8)):
+        where = gbufs[n].at[block, part]
         return pltpu.make_async_remote_copy(
-            src_ref=gbufs[n].at[block, part],
-            dst_ref=gbufs[n].at[block, part],
+            src_ref=where,
+            dst_ref=where,
             send_sem=y_send.at[n, slot],
             recv_sem=y_recv.at[n, slot],
             device_id=(c, to),
@@ -230,6 +231,48 @@
 
     all_copies = [y_copies(n) for n in range(chunks)]
 
+    def spread_copy(block, to, slot, part):
+        where = bsend.at[lax.div(block, 2), part]
+        return pltpu.make_async_remote_copy(
+            src_ref=where,
+            dst_ref=where,
+            send_sem=y_send.at[SPREAD, slot],
+            recv_sem=y_recv.at[SPREAD, slot],
+            device_id=(c, to),
+            device_id_type=MESH,
+        )
+
+    first, second = pl.ds(0, 4 * chans), pl.ds(4 * chans, 4 * chans)
+    all_copies[SPREAD].update({
+        "up low": spread_copy(t, up, 0, first),
+        "down high": spread_copy(t, down, 1, second),
+        "up high": spread_copy(t, up, 2, second),
+        "down low": spread_copy(t, down, 3, first),
+        "on low": spread_copy(down, up, 5, first),
+        "on high": spread_copy(up, down, 6, second),
+    })
+    spread_blocks = [(t, "own"), (down, "below"), (up, "above"), (far, "far")]
+
+    def spread_refs(i):
+        index = lax.div(spread_blocks[i][0], 2)
+        return bsend.at[index], brecv.at[index], chunks + i
+
+    def spread_start(i):
+        if i == 1:
+            y_arrived(SPREAD, "up high")
+        elif i == 2:
+            y_arrived(SPREAD, "down low")
+        elif i == 3:
+            y_arrived(SPREAD, "on low", "on high")
+        turn_start(*spread_refs(i))
+
+    def spread_relay(i):
+        relay(*spread_refs(i), SPREAD, spread_blocks[i][0])
+        y_start(SPREAD, spread_blocks[i][1])
+
+    def chunk_refs(n):
+        return sbuf.at[n], rbuf.at[n], n
+
     def y_start(n, *names):
         for name in names:
             all_copies[n][name].start()
@@ -265,7 +308,7 @@
         n = half * RADIX + RADIX - 1
         return pltpu.make_async_copy(gbufs[n], last_ref.at[half], out_sem.at[n])
 
-    def make_tiles(f1):
+    def make_tiles(f1, weights):
         halves = [gbufs[half * RADIX + f1] for half in range(HALVES)]
 
         @pl.loop(0, 8, step=2)
@@ -293,6 +336,8 @@
         device_id_type=MESH,
     )
 
+    half_chunks = chunks // HALVES
+
     def prepare(n):
         if n == half_chunks:
             history.wait_recv()
@@ -305,39 +350,57 @@
 
             filter_half(1)
         transform(n)
-        if n == 0:
-            pl.semaphore_wait(barrier, chans - 1 + 4)
-            history.start()
-        turn_start(n)
-
-    half_chunks = chunks // HALVES
+        turn_start(*chunk_refs(n))
+
     load_v.wait()
     load_taps.wait()
     filter_half(0)
     load_tab.wait()
-    for n in range(AHEAD):
+    transform(SPREAD)
+    pl.semaphore_wait(barrier, chans - 1 + 4)
+    y_start(SPREAD, "up low", "down high", "up high", "down low")
+    history.start()
+    normal = [n for n in range(chunks) if n != SPREAD]
+    for n in normal[:AHEAD]:
         prepare(n)
-    for n in range(chunks + 3):
-        if n < chunks:
-            relay(n)
+    weights = [
+        [pick_weights(slot_ref, blocks_ref, t * slots + slot, side, 4) for side in range(2)] for slot in range(slots)
+    ]
+
+    for step in range(len(normal) + 3):
+        if step < len(normal):
+            n = normal[step]
+            relay(*chunk_refs(n), n, t)
             start_own(n)
-        if 0 <= n - 1 < chunks:
-            start_near(n - 1)
-        if n + AHEAD < chunks:
-            prepare(n + AHEAD)
-        if 0 <= n - 2 < chunks:
-            start_far(n - 2)
-        done = n - 3
-        if 0 <= done < chunks:
-            finish(done)
-            half, f1 = done // RADIX, done % RADIX
+        if step == 0:
+            start_near(SPREAD)
+            spread_start(0)
+        if 0 <= step - 1 < len(normal):
+            start_near(normal[step - 1])
+        if step + AHEAD < len(normal):
+            prepare(normal[step + AHEAD])
+        if 1 <= step < 4:
+            spread_start(step)
+        if 0 <= step - 4 < 4:
+            spread_relay(step - 4)
+        if 0 <= step - 2 < len(normal):
+            start_far(normal[step - 2])
+        if 0 <= step - 3 < len(normal):
+            n = normal[step - 3]
+            finish(n)
+            half, f1 = n // RADIX, n % RADIX
             if f1 == RADIX - 1:
-                last_copy(half).start()
+                finish(SPREAD)
+                last_copy(0).start()
+                last_copy(1).start()
             elif half == HALVES - 1:
-                make_tiles(f1)
+                make_tiles(f1, weights)
     history.wait_send()
+    for n in normal:
+        turn_wait(sbuf.at[n], rbuf.at[n], turn_send, n)
+    for i in range(4):
+        turn_wait(bsend.at[0], brecv.at[0], turn_send, chunks + i)
     for n in range(chunks):
-        turn_wait(n, turn_send)
         for copy in all_copies[n].values():
             copy.wait_send()
     for f1 in range(RADIX - 1):
@@ -372,12 +435,14 @@
             pltpu.VMEM((RADIX, 128, 512), jnp.bfloat16),
             pltpu.VMEM((chunks, 256, 128), f32),
             pltpu.VMEM((chunks, 256, 128), f32),
+            pltpu.VMEM((tiles // 2, 256, 128), f32),
+            pltpu.VMEM((tiles // 2, 256, 128), f32),
             pltpu.VMEM((RADIX - 1, slots, 8, 2, BLOCK, BLOCK), f32),
             *[pltpu.VMEM((tiles, 8, 8, 512), f32) for _ in range(chunks)],
             pltpu.SemaphoreType.DMA((3,)),
             pltpu.SemaphoreType.DMA((2,)),
-            pltpu.SemaphoreType.DMA((chunks,)),
-            pltpu.SemaphoreType.DMA((chunks,)),
+            pltpu.SemaphoreType.DMA((chunks + 4,)),
+            pltpu.SemaphoreType.DMA((chunks + 4,)),
             pltpu.SemaphoreType.DMA((chunks, 10)),
             pltpu.SemaphoreType.DMA((chunks, 10)),
             pltpu.SemaphoreType.DMA((chunks,)),

time: 63.7 us -> 62.2 us (0.976)
  Pallas kernels: 63.6 us -> 62 us
    pallas_call x1, Pallas kernels: 59.5 us -> 58 us  [early_tiles(): pl.pallas_call(functools.partial(turn_kernel, chans, tiles, slots), out_s...]
where the time goes in v3:
time: 62.2 us; the launch traced here: 62.1 us
  Pallas kernels  62 us (100%)
    pallas_call x1, Pallas kernels, early_tiles(): pl.pallas_call(functools.partial(turn_kernel, chans, tiles, slots), out_s...  58 us
    pallas_call x1, Pallas kernels, last_tiles(): pl.pallas_call(tile_kernel, out_shape=jax.ShapeDtypeStruct((slots, 8, RAD...  4.07 us

profile of v3, /device:TPU:1, one launch (start us, length us, event | category | flops | bytes accessed | tf_op | source)
XLA Modules:
  0.0 62.1 jit_solution(16491349265505840383)
XLA Ops:
  0.0 58.0 %turn.1 = (f32[3,2,8,2,128,128]{5,4,3,2,1,0:T(8,128)S(1)}, f32[2,8,8,8,512]{4,3,2,1,0:T(8,128)S(1)}) custom-call(f32[2,8,16,1024]{3,2,1,0:T(8,128)} %v_hbm.1, f32[4,1024]{1,0:T(4,128)} %taps_hbm.1, bf16[4,2,256,512]{3,2,1,0:T(8,128)(2,1)} %constant.2.clone.tab_hbm, s32[10]{0:T(128)} %slot_ref.3, s32[2,10]{1,0:T(2,128)} %bitcast.2), custom_call_target="tpu_custom_call" | custom-call | tf_op jit(solution)/shard_map/turn/pallas_call | solution.py:422
  58.0 4.1 %tiles.1 = f32[2,8,4,2,128,128]{5,4,3,2,1,0:T(8,128)} custom-call(s32[10]{0:T(128)} %slot_ref.3, s32[2,10]{1,0:T(2,128)} %bitcast.3, f32[3,2,8,2,128,128]{5,4,3,2,1,0:T(8,128)S(1)} %get-tuple-element.7.early_ref, f32[2,8,8,8,512]{4,3,2,1,0:T(8,128)S(1)} %get-tuple-element.8.spectra_ref), custom_call_target="tpu_custom_call" | custom-call | tf_op jit(solution)/shard_map/tiles/pallas_call | solution.py:493

commit v4 on v3

--- a/solution.py
+++ b/solution.py
@@ -17,6 +17,7 @@
 LAST_LIMIT = 40 << 20
 HALVES = 2
 SPREAD = 3
+DEPTH_Z = 8
 AHEAD = 3
 
 
@@ -172,6 +173,10 @@
         else:
             sbuf[n] = spectra
 
+    def peer(across, along):
+        line = lax.rem(lax.div(c, DEPTH_Z) + across, chans // DEPTH_Z)
+        return line * DEPTH_Z + lax.rem(lax.rem(c, DEPTH_Z) + along, DEPTH_Z)
+
     def turn_copy(source, target, sem, to):
         return pltpu.make_async_remote_copy(
             src_ref=source.at[pl.ds(pl.multiple_of(to * 8, 8), 8)],
@@ -183,12 +188,15 @@
         )
 
     def turn_start(source, target, sem):
-        turn_copy(source, target, sem, lax.rem(c + chans // 2, chans)).start()
-
-        @pl.loop(1, chans // 2)
-        def _(i):
-            turn_copy(source, target, sem, lax.rem(c + i, chans)).start()
-            turn_copy(source, target, sem, lax.rem(c + chans - i, chans)).start()
+        @pl.loop(0, DEPTH_Z - 1)
+        def _(k):
+            half = lax.div(k + 1, 2)
+            along = DEPTH_Z // 2 + half - 2 * half * lax.rem(k, 2)
+            for across in (2, 1, 3, 0):
+                turn_copy(source, target, sem, peer(across, along)).start()
+
+        for across in (2, 1, 3):
+            turn_copy(source, target, sem, peer(across, 0)).start()
 
     def turn_wait(source, target, sems, sem):
         rows = pl.ds(0, (chans - 1) * 8)
@@ -349,7 +357,8 @@
                         v[ri, frame] = jnp.zeros(v.shape[2:], jnp.float32)
 
             filter_half(1)
-        transform(n)
+        if n > 0:
+            transform(n)
         turn_start(*chunk_refs(n))
 
     load_v.wait()
@@ -357,11 +366,13 @@
     filter_half(0)
     load_tab.wait()
     transform(SPREAD)
+    transform(0)
     pl.semaphore_wait(barrier, chans - 1 + 4)
+    normal = [n for n in range(chunks) if n != SPREAD]
+    prepare(normal[0])
     y_start(SPREAD, "up low", "down high", "up high", "down low")
     history.start()
-    normal = [n for n in range(chunks) if n != SPREAD]
-    for n in normal[:AHEAD]:
+    for n in normal[1:AHEAD]:
         prepare(n)
     weights = [
         [pick_weights(slot_ref, blocks_ref, t * slots + slot, side, 4) for side in range(2)] for slot in range(slots)

time: 62.2 us -> 61.7 us (level)
  no operation moved by 1% of the time
where the time goes in v4:
time: 61.7 us; the launch traced here: 61.5 us
  Pallas kernels  61.5 us (100%)
    pallas_call x1, Pallas kernels, early_tiles(): pl.pallas_call(functools.partial(turn_kernel, chans, tiles, slots), out_s...  57.5 us
    pallas_call x1, Pallas kernels, last_tiles(): pl.pallas_call(tile_kernel, out_shape=jax.ShapeDtypeStruct((slots, 8, RAD...  4.07 us

profile of v4, /device:TPU:1, one launch (start us, length us, event | category | flops | bytes accessed | tf_op | source)
XLA Modules:
  0.0 61.5 jit_solution(18155319696359544378)
XLA Ops:
  0.0 57.5 %turn.1 = (f32[3,2,8,2,128,128]{5,4,3,2,1,0:T(8,128)S(1)}, f32[2,8,8,8,512]{4,3,2,1,0:T(8,128)S(1)}) custom-call(f32[2,8,16,1024]{3,2,1,0:T(8,128)} %v_hbm.1, f32[4,1024]{1,0:T(4,128)} %taps_hbm.1, bf16[4,2,256,512]{3,2,1,0:T(8,128)(2,1)} %constant.2.clone.tab_hbm, s32[10]{0:T(128)} %slot_ref.3, s32[2,10]{1,0:T(2,128)} %bitcast.2), custom_call_target="tpu_custom_call" | custom-call | tf_op jit(solution)/shard_map/turn/pallas_call | solution.py:433
  57.5 4.1 %tiles.1 = f32[2,8,4,2,128,128]{5,4,3,2,1,0:T(8,128)} custom-call(s32[10]{0:T(128)} %slot_ref.3, s32[2,10]{1,0:T(2,128)} %bitcast.3, f32[3,2,8,2,128,128]{5,4,3,2,1,0:T(8,128)S(1)} %get-tuple-element.7.early_ref, f32[2,8,8,8,512]{4,3,2,1,0:T(8,128)S(1)} %get-tuple-element.8.spectra_ref), custom_call_target="tpu_custom_call" | custom-call | tf_op jit(solution)/shard_map/tiles/pallas_call | solution.py:504
